TPU v7x, 512 devices: a whole 4x8x8 slice. The times are simulated.
512 devices in a mesh: ctx: 128 (over y, x_lo, z), head: 4 (over x_hi, core).
Axes of the slice: x: 4 (x_hi: 2, x_lo: 2; x = x_hi * 2 + x_lo), y: 8, z: 8, core: 2. Of those that a mesh axis runs over, the one named last changes fastest.
Arguments:
- query_proj: bfloat16 [16384, 4096], P(('ctx', 'head')), may hold values from -6 to 6
- key_proj: bfloat16 [16384, 2048], P(('ctx', 'head')), may hold values from -6 to 6
- value_proj: bfloat16 [16384, 2048], P(('ctx', 'head')), may hold values from -6 to 6
- out_grad: bfloat16 [16384, 4096], P(('ctx', 'head')), may hold values from -6 to 6
Outputs:
- query_grad: bfloat16 [16384, 4096], P(('ctx', 'head'))
- key_grad: bfloat16 [16384, 2048], P(('ctx', 'head'))
- value_grad: bfloat16 [16384, 2048], P(('ctx', 'head'))
All inputs are finite; a program needn't handle non-finite values.
Results may differ from a plain program's by a relative error of at most 0.0049.
Values may be sent and summed in bfloat16 or wider, within the bound.
No kernel may reach another device: no remote copies, remote signals or barrier semaphores. Data moves between devices by JAX's collectives and lax.ppermute only.
A program may use at most 64 MiB of HBM per device.

v0:
```python
import functools
import math

import jax
import jax.numpy as jnp
from jax import lax
from jax.experimental import pallas as pl
from jax.experimental.pallas import tpu as pltpu
from jax.sharding import Mesh, PartitionSpec as P


HEAD_DIM = 256
SOFTCAP = 50.0
SCALE = 1.0 / math.sqrt(HEAD_DIM)
NAMES = ("y", "xlo", "z", "xhi", "core")
SIZES = (8, 2, 8, 2, 2)
LINES = 16
PIECE = 32
PAIR = 672
SPAN = 1536


def line_perm(steps):
    return [
        (line, line + steps) for line in range(max(0, -steps), min(LINES, LINES - steps))
    ]


def cross_perm(steps):
    return [
        (source * 2 + xhi, target * 2 + 1 - xhi)
        for source, target in line_perm(steps)
        for xhi in range(2)
    ]


SWAP = [(0, 1), (1, 0)]


def vmem_call(kernel, out_shape, args, scratch=(), flops=0, transcendentals=0, places=0, away=0, limit=16):
    spec = pl.BlockSpec(memory_space=pltpu.VMEM)
    remote = pl.BlockSpec(memory_space=pl.ANY)
    moved = sum(a.size * a.dtype.itemsize for a in jax.tree.leaves((args, out_shape)))
    return pl.pallas_call(
        kernel,
        out_shape=out_shape,
        in_specs=[pl.BlockSpec(memory_space=pltpu.SMEM)] * places
        + [remote] * away
        + [spec] * (len(args) - places - away),
        out_specs=jax.tree.map(lambda _: spec, out_shape),
        scratch_shapes=list(scratch),
        compiler_params=pltpu.CompilerParams(
            vmem_limit_bytes=limit << 20
        ),
        cost_estimate=pl.CostEstimate(
            flops=flops, bytes_accessed=moved, transcendentals=transcendentals
        ),
    )(*args)


def pack_kernel(width, left, right, out, sems):
    copies = []
    for head in range(8):
        for side, source in enumerate((left, right)):
            copies.append(
                pltpu.make_async_copy(
                    source.at[:, head * width : head * width + width],
                    out.at[head, :, side * width : side * width + width],
                    sems.at[head * 2 + side],
                )
            )
    for copy in copies:
        copy.start()
    for copy in copies:
        copy.wait()


def pack(left, right, limit=16):
    width = left.shape[1] // 8
    return vmem_call(
        functools.partial(pack_kernel, width),
        struct(8, 32, 2 * width),
        (left, right),
        scratch=[pltpu.SemaphoreType.DMA((16,))],
        away=2,
        limit=limit,
    )


def dot(left, right, contract):
    return lax.dot_general(
        left, right, (contract, ((), ())), preferred_element_type=jnp.float32
    )


def piece_rows(place, base, chunk, other_x, other_c):
    xhi = 1 - place[0] if other_x else place[0]
    core = 1 - place[1] if other_c else place[1]
    return pl.ds(pl.multiple_of(base + chunk * 128 + xhi * 64 + core * PIECE, PIECE), PIECE)


def reach_rows(place, idx, other_c):
    if idx < 8:
        return piece_rows(place, 512, idx, True, other_c)
    return piece_rows(place, 0, idx % 4, idx >= 12, other_c)


def attention_kernel(place, qg, own, partner, across, before, before_across, reach, *refs):
    query_grad, mine, mine_reach, theirs, theirs_reach = refs[:5]
    qs, gs, keys, values, scores, dweights, slopes, low_w, low_s, key_acc, value_acc = refs[5:]

    def put(rows, piece):
        keys[rows, :] = piece[:, 0:256]
        values[rows, :] = piece[:, 256:512]

    for z in range(8):
        put(piece_rows(place, 512, z, False, False), own[z])
        put(piece_rows(place, 512, z, False, True), partner[z])
        put(piece_rows(place, 512, z, True, False), across[z])
    for z in range(4):
        put(piece_rows(place, 0, z, False, False), before[z])
        put(piece_rows(place, 0, z, True, False), before_across[z])
    for idx in range(16):
        put(reach_rows(place, idx, True), reach[idx])
    for z in range(8):
        for n in range(2):
            rows = slice(z * 64 + n * PIECE, z * 64 + n * PIECE + PIECE)
            qs[rows, :] = qg[z, :, n * 256 : n * 256 + 256]
            gs[rows, :] = qg[z, :, 512 + n * 256 : 768 + n * 256]
    key_acc[...] = jnp.zeros_like(key_acc)
    value_acc[...] = jnp.zeros_like(value_acc)
    offset = place[0] * 64 + place[1] * PIECE
    column = lax.broadcasted_iota(jnp.int32, (16, 128), 1)
    token = (column // 64) * 128 + (column & 31)
    stop = token + 512
    key_row = lax.broadcasted_iota(jnp.int32, (16, 128), 0)
    for pair in range(4):
        low = 256 * pair + offset
        window = pl.ds(pl.multiple_of(low, PIECE), PAIR)
        queries = qs[pair * 128 : pair * 128 + 128, :]
        grads = gs[pair * 128 : pair * 128 + 128, :]
        scores[...] = dot(keys[window, :], queries, ((1,), (1,)))
        dweights[...] = dot(values[window, :], grads, ((1,), (1,)))
        start = jnp.maximum(token + 1, jnp.where(place[2] == 0, 512 - low, 0))

        def sums(step, carry):
            total, delta = carry
            rows = pl.ds(pl.multiple_of(step * 16, 16), 16)
            bent = jnp.tanh(scores[rows, :] * (SCALE / SOFTCAP))
            row = key_row + step * 16
            weight = jnp.where((row >= start) & (row <= stop), jnp.exp(SOFTCAP * bent), 0.0)
            scores[rows, :] = weight
            total = total + weight
            delta = delta + weight * dweights[rows, :]
            slopes[rows, :] = weight * (SCALE - SCALE * (bent * bent))
            return total, delta

        zero = jnp.zeros((16, 128), jnp.float32)
        total, delta = lax.fori_loop(0, PAIR // 16, sums, (zero, zero), unroll=21)
        inverse = 1.0 / jnp.sum(total, axis=0, keepdims=True)
        delta = jnp.sum(delta, axis=0, keepdims=True) * inverse
        inverse = jnp.broadcast_to(inverse, (16, 128))
        delta = jnp.broadcast_to(delta, (16, 128))

        def finish(step, carry):
            rows = pl.ds(pl.multiple_of(step * 16, 16), 16)
            low_w[rows, :] = (scores[rows, :] * inverse).astype(jnp.bfloat16)
            low_s[rows, :] = (slopes[rows, :] * inverse * (dweights[rows, :] - delta)).astype(
                jnp.bfloat16
            )
            return carry

        lax.fori_loop(0, PAIR // 16, finish, 0, unroll=21)
        rows_grad = dot(low_s[...], keys[window, :], ((0,), (0,))).astype(jnp.bfloat16)
        for z in range(2):
            for n in range(2):
                first = z * 64 + n * PIECE
                query_grad[pair * 2 + z, :, n * 256 : n * 256 + 256] = rows_grad[
                    first : first + PIECE, :
                ]
        key_acc[window, :] += dot(low_s[...], queries, ((1,), (0,)))
        value_acc[window, :] += dot(low_w[...], grads, ((1,), (0,)))

    def take(target, idx, rows):
        target[idx, :, 0:256] = key_acc[rows, :].astype(target.dtype)
        target[idx, :, 256:512] = value_acc[rows, :].astype(target.dtype)

    for idx in range(16):
        take(theirs_reach, idx, reach_rows(place, idx, True))
        take(mine_reach, idx, reach_rows(place, idx, False))
    for z in range(8):
        take(theirs, z, piece_rows(place, 512, z, False, True))
        take(mine, z, piece_rows(place, 512, z, False, False))


def sum_reach_kernel(mine, received, across, before, before_across):
    for idx in range(16):
        total = (mine[idx] + received[idx].astype(jnp.float32)).astype(jnp.bfloat16)
        if idx < 8:
            across[idx] = total
        elif idx < 12:
            before[idx - 8] = total
        else:
            before_across[idx - 12] = total


def sum_own_kernel(mine, partner, across, after, after_across, out):
    for z in range(8):
        total = mine[z] + partner[z].astype(jnp.float32) + across[z].astype(jnp.float32)
        if z >= 4:
            total = total + after[z - 4].astype(jnp.float32)
            total = total + after_across[z - 4].astype(jnp.float32)
        out[z] = total.astype(jnp.bfloat16)


def unpack_q_kernel(pieces, q_ref):
    for head in range(8):
        q_ref[:, head * 512 : head * 512 + 512] = pieces[head]


def unpack_kv_kernel(pieces, k_ref, v_ref):
    for head in range(8):
        k_ref[:, head * 256 : head * 256 + 256] = pieces[head, :, 0:256]
        v_ref[:, head * 256 : head * 256 + 256] = pieces[head, :, 256:512]


def struct(*dims, dtype=jnp.bfloat16):
    return jax.ShapeDtypeStruct(dims, dtype)


def exchange(value):
    return lax.all_to_all(value, "z", split_axis=0, concat_axis=0, tiled=True)


LINE, CROSS = ("y", "xlo"), ("y", "xlo", "xhi")


def shards(query_proj, key_proj, value_proj, out_grad):
    y, xlo, xhi, core = (lax.axis_index(name) for name in ("y", "xlo", "xhi", "core"))
    place = jnp.stack([xhi, core, y * 2 + xlo]).astype(jnp.int32)
    own = exchange(pack(key_proj, value_proj, limit=60))
    across = lax.ppermute(own, "xhi", SWAP)
    before = lax.ppermute(own[4:8], LINE, line_perm(1))
    before_across = lax.ppermute(own[4:8], CROSS, cross_perm(1))
    partner = lax.ppermute(own, "core", SWAP)
    qg = exchange(pack(query_proj, out_grad))
    reach = lax.ppermute(jnp.concatenate([across, before, before_across], axis=0), "core", SWAP)
    f32, bf16 = jnp.float32, jnp.bfloat16
    query_grad, mine, mine_reach, theirs, theirs_reach = vmem_call(
        attention_kernel,
        (
            struct(8, 32, 512),
            struct(8, 32, 512, dtype=f32),
            struct(16, 32, 512, dtype=f32),
            struct(8, 32, 512),
            struct(16, 32, 512),
        ),
        (place, qg, own, partner, across, before, before_across, reach),
        scratch=[
            pltpu.VMEM((512, 256), bf16),
            pltpu.VMEM((512, 256), bf16),
            pltpu.VMEM((SPAN, 256), bf16),
            pltpu.VMEM((SPAN, 256), bf16),
            pltpu.VMEM((PAIR, 128), f32),
            pltpu.VMEM((PAIR, 128), f32),
            pltpu.VMEM((PAIR, 128), f32),
            pltpu.VMEM((PAIR, 128), bf16),
            pltpu.VMEM((PAIR, 128), bf16),
            pltpu.VMEM((SPAN, 256), f32),
            pltpu.VMEM((SPAN, 256), f32),
        ],
        flops=2 * 5 * 4 * PAIR * 128 * 256,
        transcendentals=2 * 4 * PAIR * 128,
        places=1,
    )
    reach_received = lax.ppermute(theirs_reach, "core", SWAP)
    received = lax.ppermute(theirs, "core", SWAP)
    across, before, before_across = vmem_call(
        sum_reach_kernel,
        (struct(8, 32, 512), struct(4, 32, 512), struct(4, 32, 512)),
        (mine_reach, reach_received),
    )
    across = lax.ppermute(across, "xhi", SWAP)
    after = lax.ppermute(before, LINE, line_perm(-1))
    after_across = lax.ppermute(before_across, CROSS, cross_perm(-1))
    query_out = exchange(query_grad)
    kv_out = exchange(
        vmem_call(
            sum_own_kernel,
            struct(8, 32, 512),
            (mine, received, across, after, after_across),
        ),
    )
    key_out, value_out = vmem_call(
        unpack_kv_kernel, (struct(32, 2048), struct(32, 2048)), (kv_out,)
    )
    query_low = vmem_call(unpack_q_kernel, struct(32, 4096), (query_out,))
    return query_low, key_out, value_out


def solution(mesh):
    fine = Mesh(mesh.devices.reshape(SIZES), NAMES)
    spec = P(NAMES, None)
    return jax.shard_map(
        shards, mesh=fine, in_specs=(spec,) * 4, out_specs=(spec,) * 3, check_vma=False
    )
```

profile of v0, /device:TPU:32, one launch (start us, length us, event | category | flops | bytes accessed | tf_op | source)
XLA Modules:
  0.0 109.0 jit_solution(17292543736544665918)
XLA Ops:
  0.6 1.7 %shard_map.68 = bf16[8,32,512]{2,1,0:T(8,128)(2,1)} custom-call(bf16[32,2048]{1,0:T(8,128)(2,1)} %left.3, bf16[32,2048]{1,0:T(8,128)(2,1)} %right.3), custom_call_target="tpu_custom_call" | custom-call | bytes 524288 | tf_op jit(solution)/shard_map/pallas_call | solution.py:44
  2.4 0.0 copy-start
  2.4 0.0 copy-start.1
  2.4 10.5 %all-to-all-start.1 = ((bf16[8,32,512]{2,1,0:T(8,128)(2,1)}), bf16[8,32,512]{2,1,0:T(8,128)(2,1)S(1)}, u32[]{:S(2)}, u32[]{:S(2)}) async-start(bf16[8,32,512]{2,1,0:T(8,128)(2,1)} %shard_map.68), calls=%async_computation.1 | async-start | bytes 524288 | tf_op jit(solution)/shard_map/all_to_all | solution.py:232
  12.9 0.0 copy-done
  12.9 0.0 copy-done.1
  12.9 1.1 %shard_map.67 = bf16[8,32,1024]{2,1,0:T(8,128)(2,1)} custom-call(bf16[32,4096]{1,0:T(8,128)(2,1)S(1)} %copy-done, bf16[32,4096]{1,0:T(8,128)(2,1)S(1)} %copy-done.1), custom_call_target="tpu_custom_call" | custom-call | bytes 1048576 | tf_op jit(solution)/shard_map/pallas_call | solution.py:44
  14.0 10.7 %all-to-all-done.1.own = bf16[8,32,512]{2,1,0:T(8,128)(2,1)S(1)} async-done(((bf16[8,32,512]{2,1,0:T(8,128)(2,1)}), bf16[8,32,512]{2,1,0:T(8,128)(2,1)S(1)}, u32[]{:S(2)}, u32[]{:S(2)}) %all-to-all-start.1) | async-done | bytes 262176 | tf_op jit(solution)/shard_map/all_to_all | solution.py:232
  24.7 3.5 %all-to-all-start = ((bf16[8,32,1024]{2,1,0:T(8,128)(2,1)}), bf16[8,32,1024]{2,1,0:T(8,128)(2,1)S(1)}, u32[]{:S(2)}, u32[]{:S(2)}) async-start(bf16[8,32,1024]{2,1,0:T(8,128)(2,1)} %shard_map.67), calls=%async_computation | async-start | bytes 1048576 | tf_op jit(solution)/shard_map/all_to_all | solution.py:232
  28.2 4.9 %collective-permute-start.1 = (bf16[8,32,512]{2,1,0:T(8,128)(2,1)S(1)}, bf16[8,32,512]{2,1,0:T(8,128)(2,1)S(1)}, u32[]{:S(2)}, u32[]{:S(2)}) collective-permute-start(bf16[8,32,512]{2,1,0:T(8,128)(2,1)S(1)} %all-to-all-done.1.own), channel_id=1, source_target_pairs={{0,2},{2,0},{1,3},{3,1},{4,6},{6,4},{5,7},{7,5},{8,10},{10,8},{9,1... | collective-permute-start | bytes 786440 | tf_op jit(solution)/shard_map/ppermute | solution.py:242
  33.2 3.0 %collective-permute-start.3 = (bf16[4,32,512]{2,1,0:T(8,128)(2,1)S(1)}, bf16[4,32,512]{2,1,0:T(8,128)(2,1)S(1)}, u32[]{:S(2)}, u32[]{:S(2)}) collective-permute-start(bf16[4,32,512]{2,1,0:T(8,128)(2,1)S(1)} %slice.5), channel_id=1, source_target_pairs={{0,34},{2,32},{32,66},{34,64},{64,98},{66,96},{96,130},{98,128},{1... | collective-permute-start | bytes 393224 | tf_op jit(solution)/shard_map/ppermute | solution.py:244
  36.3 1.9 %collective-permute-start.2 = (bf16[4,32,512]{2,1,0:T(8,128)(2,1)S(1)}, bf16[4,32,512]{2,1,0:T(8,128)(2,1)S(1)}, u32[]{:S(2)}, u32[]{:S(2)}) collective-permute-start(bf16[4,32,512]{2,1,0:T(8,128)(2,1)S(1)} %slice.5), channel_id=1, source_target_pairs={{0,32},{32,64},{64,96},{96,128},{128,160},{160,192},{192,224},{224... | collective-permute-start | bytes 393224 | tf_op jit(solution)/shard_map/ppermute | solution.py:243
  38.2 5.5 %collective-permute-done.3.before_across = bf16[4,32,512]{2,1,0:T(8,128)(2,1)S(1)} collective-permute-done((bf16[4,32,512]{2,1,0:T(8,128)(2,1)S(1)}, bf16[4,32,512]{2,1,0:T(8,128)(2,1)S(1)}, u32[]{:S(2)}, u32[]{:S(2)}) %collective-permute-start.3) | collective-permute-done | bytes 131104 | tf_op jit(solution)/shard_map/ppermute | solution.py:244
  43.6 1.6 %collective-permute-done.2.before = bf16[4,32,512]{2,1,0:T(8,128)(2,1)S(1)} collective-permute-done((bf16[4,32,512]{2,1,0:T(8,128)(2,1)S(1)}, bf16[4,32,512]{2,1,0:T(8,128)(2,1)S(1)}, u32[]{:S(2)}, u32[]{:S(2)}) %collective-permute-start.2) | collective-permute-done | bytes 131104 | tf_op jit(solution)/shard_map/ppermute | solution.py:243
  45.2 0.0 collective-permute-done.1.across
  45.2 0.1 pad_maximum_fusion
  45.3 1.9 %collective-permute-start.4 = (bf16[16,32,512]{2,1,0:T(8,128)(2,1)S(1)}, bf16[16,32,512]{2,1,0:T(8,128)(2,1)S(1)}, u32[]{:S(2)}, u32[]{:S(2)}) collective-permute-start(bf16[16,32,512]{2,1,0:T(8,128)(2,1)S(1)} %pad_maximum_fusion), channel_id=1, source_target_pairs={{0,1},{1,0},{2,3},{3,2},{4,5},{5,4},{6,7},{7,6},{8,9},{9,8},{10,11... | collective-permute-start | bytes 1572872 | tf_op jit(solution)/shard_map/ppermute | solution.py:247
  47.2 2.4 %collective-permute-start = (bf16[8,32,512]{2,1,0:T(8,128)(2,1)S(1)}, bf16[8,32,512]{2,1,0:T(8,128)(2,1)S(1)}, u32[]{:S(2)}, u32[]{:S(2)}) collective-permute-start(bf16[8,32,512]{2,1,0:T(8,128)(2,1)S(1)} %all-to-all-done.1.own), channel_id=1, source_target_pairs={{0,1},{1,0},{2,3},{3,2},{4,5},{5,4},{6,7},{7,6},{8,9},{9,8},{10,11... | collective-permute-start | bytes 786440 | tf_op jit(solution)/shard_map/ppermute | solution.py:245
  49.6 0.1 pad_add_fusion.place
  49.7 1.1 collective-permute-done.partner
  50.8 0.0 copy-start.2
  50.8 0.7 copy-done.2
  51.5 0.0 all-to-all-done.qg
  51.5 0.0 collective-permute-done.4.reach
  51.5 0.0 copy-start.3
  51.5 0.9 copy-done.3
  52.4 5.7 %shard_map.69 = (bf16[8,32,512]{2,1,0:T(8,128)(2,1)}, f32[8,32,512]{2,1,0:T(8,128)S(1)}, f32[16,32,512]{2,1,0:T(8,128)S(1)}, bf16[8,32,512]{2,1,0:T(8,128)(2,1)S(1)}, bf16[16,32,512]{2,1,0:T(8,128)(2,1)}) custom-call(s32[3]{0:T(128)S(1)} %pad_add_fusion.place, bf16[8,32,1024]{2,1,0:T(8,128)(2,1)S(1)} %all-to-all-done.qg, ...), custom_call_target="tpu_custom_call" | custom-call | flops 880803840 | bytes 4718604 | tf_op jit(solution)/shard_map/pallas_call | solution.py:44
  58.2 0.7 copy-done.4
  58.9 2.3 %collective-permute-start.6 = (bf16[16,32,512]{2,1,0:T(8,128)(2,1)}, bf16[16,32,512]{2,1,0:T(8,128)(2,1)S(1)}, u32[]{:S(2)}, u32[]{:S(2)}) collective-permute-start(bf16[16,32,512]{2,1,0:T(8,128)(2,1)} %get-tuple-element.17), channel_id=1, source_target_pairs={{0,1},{1,0},{2,3},{3,2},{4,5},{5,4},{6,7},{7,6},{8,9},{9,8},{10,11... | collective-permute-start | bytes 1572872 | tf_op jit(solution)/shard_map/ppermute | solution.py:276
  61.1 0.0 copy-start.5
  61.1 7.3 %all-to-all-start.2 = ((bf16[8,32,512]{2,1,0:T(8,128)(2,1)}), bf16[8,32,512]{2,1,0:T(8,128)(2,1)S(1)}, u32[]{:S(2)}, u32[]{:S(2)}) async-start(bf16[8,32,512]{2,1,0:T(8,128)(2,1)} %get-tuple-element.13), calls=%async_computation.2 | async-start | bytes 524288 | tf_op jit(solution)/shard_map/all_to_all | solution.py:232
  68.4 0.0 copy-done.5
  68.4 1.9 %collective-permute-start.5 = (bf16[8,32,512]{2,1,0:T(8,128)(2,1)S(1)}, bf16[8,32,512]{2,1,0:T(8,128)(2,1)S(1)}, u32[]{:S(2)}, u32[]{:S(2)}) collective-permute-start(bf16[8,32,512]{2,1,0:T(8,128)(2,1)S(1)} %copy-done.5), channel_id=1, source_target_pairs={{0,1},{1,0},{2,3},{3,2},{4,5},{5,4},{6,7},{7,6},{8,9},{9,8},{10,11... | collective-permute-start | bytes 786440 | tf_op jit(solution)/shard_map/ppermute | solution.py:277
  70.3 0.0 collective-permute-done.6.received
  70.3 0.1 shard_map.71
  70.4 3.5 %collective-permute-start.7 = (bf16[8,32,512]{2,1,0:T(8,128)(2,1)S(1)}, bf16[8,32,512]{2,1,0:T(8,128)(2,1)S(1)}, u32[]{:S(2)}, u32[]{:S(2)}) collective-permute-start(bf16[8,32,512]{2,1,0:T(8,128)(2,1)S(1)} %get-tuple-element.18), channel_id=1, source_target_pairs={{0,2},{2,0},{1,3},{3,1},{4,6},{6,4},{5,7},{7,5},{8,10},{10,8},{9,1... | collective-permute-start | bytes 786440 | tf_op jit(solution)/shard_map/ppermute | solution.py:283
  73.9 3.3 %collective-permute-start.8 = (bf16[4,32,512]{2,1,0:T(8,128)(2,1)S(1)}, bf16[4,32,512]{2,1,0:T(8,128)(2,1)S(1)}, u32[]{:S(2)}, u32[]{:S(2)}) collective-permute-start(bf16[4,32,512]{2,1,0:T(8,128)(2,1)S(1)} %get-tuple-element.19), channel_id=1, source_target_pairs={{32,0},{64,32},{96,64},{128,96},{160,128},{192,160},{224,192},{256... | collective-permute-start | bytes 393224 | tf_op jit(solution)/shard_map/ppermute | solution.py:284
  77.2 1.9 %collective-permute-start.9 = (bf16[4,32,512]{2,1,0:T(8,128)(2,1)S(1)}, bf16[4,32,512]{2,1,0:T(8,128)(2,1)S(1)}, u32[]{:S(2)}, u32[]{:S(2)}) collective-permute-start(bf16[4,32,512]{2,1,0:T(8,128)(2,1)S(1)} %get-tuple-element.20), channel_id=1, source_target_pairs={{32,2},{34,0},{64,34},{66,32},{96,66},{98,64},{128,98},{130,96},{1... | collective-permute-start | bytes 393224 | tf_op jit(solution)/shard_map/ppermute | solution.py:285
  79.2 0.0 collective-permute-done.5.partner
  79.2 3.6 %collective-permute-done.8.after = bf16[4,32,512]{2,1,0:T(8,128)(2,1)S(1)} collective-permute-done((bf16[4,32,512]{2,1,0:T(8,128)(2,1)S(1)}, bf16[4,32,512]{2,1,0:T(8,128)(2,1)S(1)}, u32[]{:S(2)}, u32[]{:S(2)}) %collective-permute-start.8) | collective-permute-done | bytes 131104 | tf_op jit(solution)/shard_map/ppermute | solution.py:284
  82.8 5.4 %collective-permute-done.9.after_across = bf16[4,32,512]{2,1,0:T(8,128)(2,1)S(1)} collective-permute-done((bf16[4,32,512]{2,1,0:T(8,128)(2,1)S(1)}, bf16[4,32,512]{2,1,0:T(8,128)(2,1)S(1)}, u32[]{:S(2)}, u32[]{:S(2)}) %collective-permute-start.9) | collective-permute-done | bytes 131104 | tf_op jit(solution)/shard_map/ppermute | solution.py:285
  88.2 0.0 collective-permute-done.7.across
  88.2 0.8 shard_map.72
  89.0 0.0 all-to-all-done.2.pieces
  89.0 7.2 %all-to-all-start.3 = ((bf16[8,32,512]{2,1,0:T(8,128)(2,1)}), bf16[8,32,512]{2,1,0:T(8,128)(2,1)S(1)}, u32[]{:S(2)}, u32[]{:S(2)}) async-start(bf16[8,32,512]{2,1,0:T(8,128)(2,1)} %shard_map.72), calls=%async_computation.3 | async-start | bytes 524288 | tf_op jit(solution)/shard_map/all_to_all | solution.py:232
  96.2 0.7 shard_map.70
  96.9 11.3 %all-to-all-done.3.pieces = bf16[8,32,512]{2,1,0:T(8,128)(2,1)S(1)} async-done(((bf16[8,32,512]{2,1,0:T(8,128)(2,1)}), bf16[8,32,512]{2,1,0:T(8,128)(2,1)S(1)}, u32[]{:S(2)}, u32[]{:S(2)}) %all-to-all-start.3) | async-done | bytes 262176 | tf_op jit(solution)/shard_map/all_to_all | solution.py:232
  108.2 0.7 shard_map.73
  (2 shorter events, 0.0 us)
Async XLA Ops:
  2.4 10.5 %copy-start = (bf16[32,4096]{1,0:T(8,128)(2,1)S(1)}, bf16[32,4096]{1,0:T(8,128)(2,1)}, u32[]{:S(2)}) copy-start(bf16[32,4096]{1,0:T(8,128)(2,1)} %left.2) | copy-start | bytes 786436
  2.4 10.5 %copy-start.1 = (bf16[32,4096]{1,0:T(8,128)(2,1)S(1)}, bf16[32,4096]{1,0:T(8,128)(2,1)}, u32[]{:S(2)}) copy-start(bf16[32,4096]{1,0:T(8,128)(2,1)} %right.2) | copy-start | bytes 786436
  2.4 22.3 %all-to-all-start.1 = ((bf16[8,32,512]{2,1,0:T(8,128)(2,1)}), bf16[8,32,512]{2,1,0:T(8,128)(2,1)S(1)}, u32[]{:S(2)}, u32[]{:S(2)}) async-start(bf16[8,32,512]{2,1,0:T(8,128)(2,1)} %shard_map.68), calls=%async_computation.1 | async-start | bytes 524288 | tf_op jit(solution)/shard_map/all_to_all | solution.py:232
  24.7 26.7 %all-to-all-start = ((bf16[8,32,1024]{2,1,0:T(8,128)(2,1)}), bf16[8,32,1024]{2,1,0:T(8,128)(2,1)S(1)}, u32[]{:S(2)}, u32[]{:S(2)}) async-start(bf16[8,32,1024]{2,1,0:T(8,128)(2,1)} %shard_map.67), calls=%async_computation | async-start | bytes 1048576 | tf_op jit(solution)/shard_map/all_to_all | solution.py:232
  28.2 17.0 %collective-permute-start.1 = (bf16[8,32,512]{2,1,0:T(8,128)(2,1)S(1)}, bf16[8,32,512]{2,1,0:T(8,128)(2,1)S(1)}, u32[]{:S(2)}, u32[]{:S(2)}) collective-permute-start(bf16[8,32,512]{2,1,0:T(8,128)(2,1)S(1)} %all-to-all-done.1.own), channel_id=1, source_target_pairs={{0,2},{2,0},{1,3},{3,1},{4,6},{6,4},{5,7},{7,5},{8,10},{10,8},{9,1... | collective-permute-start | bytes 786440 | tf_op jit(solution)/shard_map/ppermute | solution.py:242
  33.2 10.4 %collective-permute-start.3 = (bf16[4,32,512]{2,1,0:T(8,128)(2,1)S(1)}, bf16[4,32,512]{2,1,0:T(8,128)(2,1)S(1)}, u32[]{:S(2)}, u32[]{:S(2)}) collective-permute-start(bf16[4,32,512]{2,1,0:T(8,128)(2,1)S(1)} %slice.5), channel_id=1, source_target_pairs={{0,34},{2,32},{32,66},{34,64},{64,98},{66,96},{96,130},{98,128},{1... | collective-permute-start | bytes 393224 | tf_op jit(solution)/shard_map/ppermute | solution.py:244
  36.3 9.0 %collective-permute-start.2 = (bf16[4,32,512]{2,1,0:T(8,128)(2,1)S(1)}, bf16[4,32,512]{2,1,0:T(8,128)(2,1)S(1)}, u32[]{:S(2)}, u32[]{:S(2)}) collective-permute-start(bf16[4,32,512]{2,1,0:T(8,128)(2,1)S(1)} %slice.5), channel_id=1, source_target_pairs={{0,32},{32,64},{64,96},{96,128},{128,160},{160,192},{192,224},{224... | collective-permute-start | bytes 393224 | tf_op jit(solution)/shard_map/ppermute | solution.py:243
  45.3 6.2 %collective-permute-start.4 = (bf16[16,32,512]{2,1,0:T(8,128)(2,1)S(1)}, bf16[16,32,512]{2,1,0:T(8,128)(2,1)S(1)}, u32[]{:S(2)}, u32[]{:S(2)}) collective-permute-start(bf16[16,32,512]{2,1,0:T(8,128)(2,1)S(1)} %pad_maximum_fusion), channel_id=1, source_target_pairs={{0,1},{1,0},{2,3},{3,2},{4,5},{5,4},{6,7},{7,6},{8,9},{9,8},{10,11... | collective-permute-start | bytes 1572872 | tf_op jit(solution)/shard_map/ppermute | solution.py:247
  47.2 3.6 %collective-permute-start = (bf16[8,32,512]{2,1,0:T(8,128)(2,1)S(1)}, bf16[8,32,512]{2,1,0:T(8,128)(2,1)S(1)}, u32[]{:S(2)}, u32[]{:S(2)}) collective-permute-start(bf16[8,32,512]{2,1,0:T(8,128)(2,1)S(1)} %all-to-all-done.1.own), channel_id=1, source_target_pairs={{0,1},{1,0},{2,3},{3,2},{4,5},{5,4},{6,7},{7,6},{8,9},{9,8},{10,11... | collective-permute-start | bytes 786440 | tf_op jit(solution)/shard_map/ppermute | solution.py:245
  50.8 0.7 copy-start.2
  51.5 1.0 copy-start.3
  58.2 0.7 copy-start.4
  58.9 11.5 %collective-permute-start.6 = (bf16[16,32,512]{2,1,0:T(8,128)(2,1)}, bf16[16,32,512]{2,1,0:T(8,128)(2,1)S(1)}, u32[]{:S(2)}, u32[]{:S(2)}) collective-permute-start(bf16[16,32,512]{2,1,0:T(8,128)(2,1)} %get-tuple-element.17), channel_id=1, source_target_pairs={{0,1},{1,0},{2,3},{3,2},{4,5},{5,4},{6,7},{7,6},{8,9},{9,8},{10,11... | collective-permute-start | bytes 1572872 | tf_op jit(solution)/shard_map/ppermute | solution.py:276
  61.1 7.3 %copy-start.5 = (bf16[8,32,512]{2,1,0:T(8,128)(2,1)S(1)}, bf16[8,32,512]{2,1,0:T(8,128)(2,1)}, u32[]{:S(2)}) copy-start(bf16[8,32,512]{2,1,0:T(8,128)(2,1)} %copy-done.4) | copy-start | bytes 786436
  61.1 27.8 %all-to-all-start.2 = ((bf16[8,32,512]{2,1,0:T(8,128)(2,1)}), bf16[8,32,512]{2,1,0:T(8,128)(2,1)S(1)}, u32[]{:S(2)}, u32[]{:S(2)}) async-start(bf16[8,32,512]{2,1,0:T(8,128)(2,1)} %get-tuple-element.13), calls=%async_computation.2 | async-start | bytes 524288 | tf_op jit(solution)/shard_map/all_to_all | solution.py:232
  68.4 10.8 %collective-permute-start.5 = (bf16[8,32,512]{2,1,0:T(8,128)(2,1)S(1)}, bf16[8,32,512]{2,1,0:T(8,128)(2,1)S(1)}, u32[]{:S(2)}, u32[]{:S(2)}) collective-permute-start(bf16[8,32,512]{2,1,0:T(8,128)(2,1)S(1)} %copy-done.5), channel_id=1, source_target_pairs={{0,1},{1,0},{2,3},{3,2},{4,5},{5,4},{6,7},{7,6},{8,9},{9,8},{10,11... | collective-permute-start | bytes 786440 | tf_op jit(solution)/shard_map/ppermute | solution.py:277
  70.4 17.7 %collective-permute-start.7 = (bf16[8,32,512]{2,1,0:T(8,128)(2,1)S(1)}, bf16[8,32,512]{2,1,0:T(8,128)(2,1)S(1)}, u32[]{:S(2)}, u32[]{:S(2)}) collective-permute-start(bf16[8,32,512]{2,1,0:T(8,128)(2,1)S(1)} %get-tuple-element.18), channel_id=1, source_target_pairs={{0,2},{2,0},{1,3},{3,1},{4,6},{6,4},{5,7},{7,5},{8,10},{10,8},{9,1... | collective-permute-start | bytes 786440 | tf_op jit(solution)/shard_map/ppermute | solution.py:283
  73.9 8.9 %collective-permute-start.8 = (bf16[4,32,512]{2,1,0:T(8,128)(2,1)S(1)}, bf16[4,32,512]{2,1,0:T(8,128)(2,1)S(1)}, u32[]{:S(2)}, u32[]{:S(2)}) collective-permute-start(bf16[4,32,512]{2,1,0:T(8,128)(2,1)S(1)} %get-tuple-element.19), channel_id=1, source_target_pairs={{32,0},{64,32},{96,64},{128,96},{160,128},{192,160},{224,192},{256... | collective-permute-start | bytes 393224 | tf_op jit(solution)/shard_map/ppermute | solution.py:284
  77.2 10.9 %collective-permute-start.9 = (bf16[4,32,512]{2,1,0:T(8,128)(2,1)S(1)}, bf16[4,32,512]{2,1,0:T(8,128)(2,1)S(1)}, u32[]{:S(2)}, u32[]{:S(2)}) collective-permute-start(bf16[4,32,512]{2,1,0:T(8,128)(2,1)S(1)} %get-tuple-element.20), channel_id=1, source_target_pairs={{32,2},{34,0},{64,34},{66,32},{96,66},{98,64},{128,98},{130,96},{1... | collective-permute-start | bytes 393224 | tf_op jit(solution)/shard_map/ppermute | solution.py:285
  89.0 19.3 %all-to-all-start.3 = ((bf16[8,32,512]{2,1,0:T(8,128)(2,1)}), bf16[8,32,512]{2,1,0:T(8,128)(2,1)S(1)}, u32[]{:S(2)}, u32[]{:S(2)}) async-start(bf16[8,32,512]{2,1,0:T(8,128)(2,1)} %shard_map.72), calls=%async_computation.3 | async-start | bytes 524288 | tf_op jit(solution)/shard_map/all_to_all | solution.py:232
where the time goes:
time: 110 us; the launch traced here: 109 us
  starting transfers between devices  55.5 us (50%)
  waiting for transfers between devices  39.2 us (36%)
  Pallas kernels  10.9 us (10%)
  local copies, waits for them, and re-layouts  2.37 us (2%)
    all_to_all x4, starting transfers between devices, exchange(): return lax.all_to_all(value, 'z', split_axis=0, concat_axis=0, tiled=True)  28.4 us
    all_to_all x4, waiting for transfers between devices, exchange(): return lax.all_to_all(value, 'z', split_axis=0, concat_axis=0, tiled=True)  22.1 us
    pallas_call x7, Pallas kernels, vmem_call(): pl.pallas_call(kernel, out_shape=out_shape, in_specs=[pl.BlockSpec(memory...  10.9 us
    ppermute x1, waiting for transfers between devices, shards(): before_across = lax.ppermute(own[4:8], CROSS, cross_perm(1))  5.45 us
    ppermute x1, waiting for transfers between devices, shards(): after_across = lax.ppermute(before_across, CROSS, cross_perm(-1))  5.38 us
    ppermute x1, starting transfers between devices, shards(): across = lax.ppermute(own, 'xhi', SWAP)  4.93 us
    ppermute x1, waiting for transfers between devices, shards(): after = lax.ppermute(before, LINE, line_perm(-1))  3.62 us
    ppermute x1, starting transfers between devices, shards(): across = lax.ppermute(across, 'xhi', SWAP)  3.45 us
  transfers between devices with their start and end apart: 14, of which 7 were waited for; matrix products, arithmetic and copies ran while one was open for 0% of the time, Pallas kernels for 3%

commit v1 on v0

--- a/solution.py
+++ b/solution.py
@@ -17,6 +17,7 @@
 LINES = 16
 PIECE = 32
 PAIR = 672
+SHARED = PAIR - 256
 SPAN = 1536
 
 
@@ -127,8 +128,9 @@
             rows = slice(z * 64 + n * PIECE, z * 64 + n * PIECE + PIECE)
             qs[rows, :] = qg[z, :, n * 256 : n * 256 + 256]
             gs[rows, :] = qg[z, :, 512 + n * 256 : 768 + n * 256]
-    key_acc[...] = jnp.zeros_like(key_acc)
-    value_acc[...] = jnp.zeros_like(value_acc)
+    for acc in (key_acc, value_acc):
+        acc[0:96, :] = jnp.zeros((96, 256), jnp.float32)
+        acc[1440:SPAN, :] = jnp.zeros((96, 256), jnp.float32)
     offset = place[0] * 64 + place[1] * PIECE
     column = lax.broadcasted_iota(jnp.int32, (16, 128), 1)
     token = (column // 64) * 128 + (column & 31)
@@ -143,12 +145,11 @@
         dweights[...] = dot(values[window, :], grads, ((1,), (1,)))
         start = jnp.maximum(token + 1, jnp.where(place[2] == 0, 512 - low, 0))
 
-        def sums(step, carry):
+        def sums(allowed, step, carry):
             total, delta = carry
             rows = pl.ds(pl.multiple_of(step * 16, 16), 16)
             bent = jnp.tanh(scores[rows, :] * (SCALE / SOFTCAP))
-            row = key_row + step * 16
-            weight = jnp.where((row >= start) & (row <= stop), jnp.exp(SOFTCAP * bent), 0.0)
+            weight = jnp.where(allowed(key_row + step * 16), jnp.exp(SOFTCAP * bent), 0.0)
             scores[rows, :] = weight
             total = total + weight
             delta = delta + weight * dweights[rows, :]
@@ -156,7 +157,10 @@
             return total, delta
 
         zero = jnp.zeros((16, 128), jnp.float32)
-        total, delta = lax.fori_loop(0, PAIR // 16, sums, (zero, zero), unroll=21)
+        early = functools.partial(sums, lambda row: row >= start)
+        late = functools.partial(sums, lambda row: row <= stop)
+        total, delta = lax.fori_loop(0, 32, early, (zero, zero), unroll=16)
+        total, delta = lax.fori_loop(32, PAIR // 16, late, (total, delta), unroll=10)
         inverse = 1.0 / jnp.sum(total, axis=0, keepdims=True)
         delta = jnp.sum(delta, axis=0, keepdims=True) * inverse
         inverse = jnp.broadcast_to(inverse, (16, 128))
@@ -178,8 +182,15 @@
                 query_grad[pair * 2 + z, :, n * 256 : n * 256 + 256] = rows_grad[
                     first : first + PIECE, :
                 ]
-        key_acc[window, :] += dot(low_s[...], queries, ((1,), (0,)))
-        value_acc[window, :] += dot(low_w[...], grads, ((1,), (0,)))
+        for acc, terms in (
+            (key_acc, dot(low_s[...], queries, ((1,), (0,)))),
+            (value_acc, dot(low_w[...], grads, ((1,), (0,)))),
+        ):
+            if pair == 0:
+                acc[window, :] = terms
+            else:
+                acc[pl.ds(pl.multiple_of(low, PIECE), SHARED), :] += terms[0:SHARED, :]
+                acc[pl.ds(pl.multiple_of(low + SHARED, PIECE), 256), :] = terms[SHARED:PAIR, :]
 
     def take(target, idx, rows):
         target[idx, :, 0:256] = key_acc[rows, :].astype(target.dtype)
@@ -204,24 +215,21 @@
             before_across[idx - 12] = total
 
 
-def sum_own_kernel(mine, partner, across, after, after_across, out):
+def sum_own_kernel(query_grad, mine, partner, across, after, after_across, out):
+    out[:, :, 0:512] = query_grad[...]
     for z in range(8):
         total = mine[z] + partner[z].astype(jnp.float32) + across[z].astype(jnp.float32)
         if z >= 4:
             total = total + after[z - 4].astype(jnp.float32)
             total = total + after_across[z - 4].astype(jnp.float32)
-        out[z] = total.astype(jnp.bfloat16)
-
-
-def unpack_q_kernel(pieces, q_ref):
+        out[z, :, 512:1024] = total.astype(jnp.bfloat16)
+
+
+def unpack_kernel(pieces, q_ref, k_ref, v_ref):
     for head in range(8):
-        q_ref[:, head * 512 : head * 512 + 512] = pieces[head]
-
-
-def unpack_kv_kernel(pieces, k_ref, v_ref):
-    for head in range(8):
-        k_ref[:, head * 256 : head * 256 + 256] = pieces[head, :, 0:256]
-        v_ref[:, head * 256 : head * 256 + 256] = pieces[head, :, 256:512]
+        q_ref[:, head * 512 : head * 512 + 512] = pieces[head, :, 0:512]
+        k_ref[:, head * 256 : head * 256 + 256] = pieces[head, :, 512:768]
+        v_ref[:, head * 256 : head * 256 + 256] = pieces[head, :, 768:1024]
 
 
 def struct(*dims, dtype=jnp.bfloat16):
@@ -283,19 +291,16 @@
     across = lax.ppermute(across, "xhi", SWAP)
     after = lax.ppermute(before, LINE, line_perm(-1))
     after_across = lax.ppermute(before_across, CROSS, cross_perm(-1))
-    query_out = exchange(query_grad)
-    kv_out = exchange(
+    pieces = exchange(
         vmem_call(
             sum_own_kernel,
-            struct(8, 32, 512),
-            (mine, received, across, after, after_across),
+            struct(8, 32, 1024),
+            (query_grad, mine, received, across, after, after_across),
         ),
     )
-    key_out, value_out = vmem_call(
-        unpack_kv_kernel, (struct(32, 2048), struct(32, 2048)), (kv_out,)
-    )
-    query_low = vmem_call(unpack_q_kernel, struct(32, 4096), (query_out,))
-    return query_low, key_out, value_out
+    return vmem_call(
+        unpack_kernel, (struct(32, 4096), struct(32, 2048), struct(32, 2048)), (pieces,)
+    )
 
 
 def solution(mesh):

time: 110 us -> 104 us (0.945)
  blocking collectives: 0 us -> 24.6 us
  starting transfers between devices: 55.5 us -> 41.2 us
  waiting for transfers between devices: 39.2 us -> 27.7 us
  local copies, waits for them, and re-layouts: 2.37 us -> 0.02 us
  Pallas kernels: 10.9 us -> 8.56 us
    all_to_all x0 -> x1, blocking collectives: none -> 24.6 us  [exchange(): return lax.all_to_all(value, 'z', split_axis=0, concat_axis=0, tiled=True)]
    all_to_all x4 -> x2, starting transfers between devices: 28.4 us -> 14 us  [exchange(): return lax.all_to_all(value, 'z', split_axis=0, concat_axis=0, tiled=True)]
    all_to_all x4 -> x2, waiting for transfers between devices: 22.1 us -> 10.7 us  [exchange(): return lax.all_to_all(value, 'z', split_axis=0, concat_axis=0, tiled=True)]
    pallas_call x7 -> x6, Pallas kernels: 10.9 us -> 8.56 us  [vmem_call(): pl.pallas_call(kernel, out_shape=out_shape, in_specs=[pl.BlockSpec(memory...]
    unnamed x12 -> x4, local copies, waits for them, and re-layouts: 2.36 us -> 0.01 us
  transfers between devices with their start and end apart: 14 -> 12, of which waited for: 7 -> 6; matrix products, arithmetic and copies ran while one was open for 0% -> 0% of each run, Pallas kernels for 3% -> 1%
where the time goes in v1:
time: 104 us; the launch traced here: 103 us
  starting transfers between devices  41.2 us (40%)
  waiting for transfers between devices  27.7 us (27%)
  blocking collectives  24.6 us (24%)
  Pallas kernels  8.56 us (8%)
    all_to_all x1, blocking collectives, exchange(): return lax.all_to_all(value, 'z', split_axis=0, concat_axis=0, tiled=True)  24.6 us
    all_to_all x2, starting transfers between devices, exchange(): return lax.all_to_all(value, 'z', split_axis=0, concat_axis=0, tiled=True)  14 us
    all_to_all x2, waiting for transfers between devices, exchange(): return lax.all_to_all(value, 'z', split_axis=0, concat_axis=0, tiled=True)  10.7 us
    pallas_call x6, Pallas kernels, vmem_call(): pl.pallas_call(kernel, out_shape=out_shape, in_specs=[pl.BlockSpec(memory...  8.56 us
    ppermute x1, waiting for transfers between devices, shards(): before_across = lax.ppermute(own[4:8], CROSS, cross_perm(1))  5.45 us
    ppermute x1, waiting for transfers between devices, shards(): after_across = lax.ppermute(before_across, CROSS, cross_perm(-1))  5.38 us
    ppermute x1, starting transfers between devices, shards(): across = lax.ppermute(own, 'xhi', SWAP)  4.93 us
    ppermute x1, waiting for transfers between devices, shards(): after = lax.ppermute(before, LINE, line_perm(-1))  3.49 us
  transfers between devices with their start and end apart: 12, of which 6 were waited for; matrix products, arithmetic and copies ran while one was open for 0% of the time, Pallas kernels for 1%

profile of v1, /device:TPU:32, one launch (start us, length us, event | category | flops | bytes accessed | tf_op | source)
XLA Modules:
  0.0 103.0 jit_solution(5776118901990580658)
XLA Ops:
  0.6 1.7 %shard_map.68 = bf16[8,32,512]{2,1,0:T(8,128)(2,1)} custom-call(bf16[32,2048]{1,0:T(8,128)(2,1)} %left.3, bf16[32,2048]{1,0:T(8,128)(2,1)} %right.3), custom_call_target="tpu_custom_call" | custom-call | bytes 524288 | tf_op jit(solution)/shard_map/pallas_call | solution.py:45
  2.4 0.0 copy-start
  2.4 0.0 copy-start.1
  2.4 10.5 %all-to-all-start.1 = ((bf16[8,32,512]{2,1,0:T(8,128)(2,1)}), bf16[8,32,512]{2,1,0:T(8,128)(2,1)S(1)}, u32[]{:S(2)}, u32[]{:S(2)}) async-start(bf16[8,32,512]{2,1,0:T(8,128)(2,1)} %shard_map.68), calls=%async_computation.1 | async-start | bytes 524288 | tf_op jit(solution)/shard_map/all_to_all | solution.py:240
  12.9 0.0 copy-done
  12.9 0.0 copy-done.1
  12.9 1.1 %shard_map.67 = bf16[8,32,1024]{2,1,0:T(8,128)(2,1)} custom-call(bf16[32,4096]{1,0:T(8,128)(2,1)S(1)} %copy-done, bf16[32,4096]{1,0:T(8,128)(2,1)S(1)} %copy-done.1), custom_call_target="tpu_custom_call" | custom-call | bytes 1048576 | tf_op jit(solution)/shard_map/pallas_call | solution.py:45
  14.0 10.7 %all-to-all-done.1.own = bf16[8,32,512]{2,1,0:T(8,128)(2,1)S(1)} async-done(((bf16[8,32,512]{2,1,0:T(8,128)(2,1)}), bf16[8,32,512]{2,1,0:T(8,128)(2,1)S(1)}, u32[]{:S(2)}, u32[]{:S(2)}) %all-to-all-start.1) | async-done | bytes 262176 | tf_op jit(solution)/shard_map/all_to_all | solution.py:240
  24.7 3.5 %all-to-all-start = ((bf16[8,32,1024]{2,1,0:T(8,128)(2,1)}), bf16[8,32,1024]{2,1,0:T(8,128)(2,1)S(1)}, u32[]{:S(2)}, u32[]{:S(2)}) async-start(bf16[8,32,1024]{2,1,0:T(8,128)(2,1)} %shard_map.67), calls=%async_computation | async-start | bytes 1048576 | tf_op jit(solution)/shard_map/all_to_all | solution.py:240
  28.2 4.9 %collective-permute-start.1 = (bf16[8,32,512]{2,1,0:T(8,128)(2,1)S(1)}, bf16[8,32,512]{2,1,0:T(8,128)(2,1)S(1)}, u32[]{:S(2)}, u32[]{:S(2)}) collective-permute-start(bf16[8,32,512]{2,1,0:T(8,128)(2,1)S(1)} %all-to-all-done.1.own), channel_id=1, source_target_pairs={{0,2},{2,0},{1,3},{3,1},{4,6},{6,4},{5,7},{7,5},{8,10},{10,8},{9,1... | collective-permute-start | bytes 786440 | tf_op jit(solution)/shard_map/ppermute | solution.py:250
  33.2 3.0 %collective-permute-start.3 = (bf16[4,32,512]{2,1,0:T(8,128)(2,1)S(1)}, bf16[4,32,512]{2,1,0:T(8,128)(2,1)S(1)}, u32[]{:S(2)}, u32[]{:S(2)}) collective-permute-start(bf16[4,32,512]{2,1,0:T(8,128)(2,1)S(1)} %slice.5), channel_id=1, source_target_pairs={{0,34},{2,32},{32,66},{34,64},{64,98},{66,96},{96,130},{98,128},{1... | collective-permute-start | bytes 393224 | tf_op jit(solution)/shard_map/ppermute | solution.py:252
  36.3 1.9 %collective-permute-start.2 = (bf16[4,32,512]{2,1,0:T(8,128)(2,1)S(1)}, bf16[4,32,512]{2,1,0:T(8,128)(2,1)S(1)}, u32[]{:S(2)}, u32[]{:S(2)}) collective-permute-start(bf16[4,32,512]{2,1,0:T(8,128)(2,1)S(1)} %slice.5), channel_id=1, source_target_pairs={{0,32},{32,64},{64,96},{96,128},{128,160},{160,192},{192,224},{224... | collective-permute-start | bytes 393224 | tf_op jit(solution)/shard_map/ppermute | solution.py:251
  38.2 5.5 %collective-permute-done.3.before_across = bf16[4,32,512]{2,1,0:T(8,128)(2,1)S(1)} collective-permute-done((bf16[4,32,512]{2,1,0:T(8,128)(2,1)S(1)}, bf16[4,32,512]{2,1,0:T(8,128)(2,1)S(1)}, u32[]{:S(2)}, u32[]{:S(2)}) %collective-permute-start.3) | collective-permute-done | bytes 131104 | tf_op jit(solution)/shard_map/ppermute | solution.py:252
  43.6 1.6 %collective-permute-done.2.before = bf16[4,32,512]{2,1,0:T(8,128)(2,1)S(1)} collective-permute-done((bf16[4,32,512]{2,1,0:T(8,128)(2,1)S(1)}, bf16[4,32,512]{2,1,0:T(8,128)(2,1)S(1)}, u32[]{:S(2)}, u32[]{:S(2)}) %collective-permute-start.2) | collective-permute-done | bytes 131104 | tf_op jit(solution)/shard_map/ppermute | solution.py:251
  45.2 0.0 collective-permute-done.1.across
  45.2 0.1 pad_maximum_fusion
  45.3 1.9 %collective-permute-start.4 = (bf16[16,32,512]{2,1,0:T(8,128)(2,1)S(1)}, bf16[16,32,512]{2,1,0:T(8,128)(2,1)S(1)}, u32[]{:S(2)}, u32[]{:S(2)}) collective-permute-start(bf16[16,32,512]{2,1,0:T(8,128)(2,1)S(1)} %pad_maximum_fusion), channel_id=1, source_target_pairs={{0,1},{1,0},{2,3},{3,2},{4,5},{5,4},{6,7},{7,6},{8,9},{9,8},{10,11... | collective-permute-start | bytes 1572872 | tf_op jit(solution)/shard_map/ppermute | solution.py:255
  47.2 2.4 %collective-permute-start = (bf16[8,32,512]{2,1,0:T(8,128)(2,1)S(1)}, bf16[8,32,512]{2,1,0:T(8,128)(2,1)S(1)}, u32[]{:S(2)}, u32[]{:S(2)}) collective-permute-start(bf16[8,32,512]{2,1,0:T(8,128)(2,1)S(1)} %all-to-all-done.1.own), channel_id=1, source_target_pairs={{0,1},{1,0},{2,3},{3,2},{4,5},{5,4},{6,7},{7,6},{8,9},{9,8},{10,11... | collective-permute-start | bytes 786440 | tf_op jit(solution)/shard_map/ppermute | solution.py:253
  49.6 0.1 pad_add_fusion.place
  49.7 1.1 %collective-permute-done.partner = bf16[8,32,512]{2,1,0:T(8,128)(2,1)S(1)} collective-permute-done((bf16[8,32,512]{2,1,0:T(8,128)(2,1)S(1)}, bf16[8,32,512]{2,1,0:T(8,128)(2,1)S(1)}, u32[]{:S(2)}, u32[]{:S(2)}) %collective-permute-start) | collective-permute-done | bytes 262176 | tf_op jit(solution)/shard_map/ppermute | solution.py:253
  50.8 0.0 all-to-all-done.qg
  50.8 0.0 collective-permute-done.4.reach
  50.8 4.7 %shard_map.69 = (bf16[8,32,512]{2,1,0:T(8,128)(2,1)S(1)}, f32[8,32,512]{2,1,0:T(8,128)S(1)}, f32[16,32,512]{2,1,0:T(8,128)S(1)}, bf16[8,32,512]{2,1,0:T(8,128)(2,1)S(1)}, bf16[16,32,512]{2,1,0:T(8,128)(2,1)S(1)}) custom-call(s32[3]{0:T(128)S(1)} %pad_add_fusion.place, bf16[8,32,1024]{2,1,0:T(8,128)(2,1)S(1)} %all-to-all-done.qg, ...), custom_call_target="tpu_custom_call" | custom-call | flops 880803840 | bytes 4718604 | tf_op jit(solution)/shard_map/pallas_call | solution.py:45
  55.4 2.3 %collective-permute-start.6 = (bf16[16,32,512]{2,1,0:T(8,128)(2,1)S(1)}, bf16[16,32,512]{2,1,0:T(8,128)(2,1)S(1)}, u32[]{:S(2)}, u32[]{:S(2)}) collective-permute-start(bf16[16,32,512]{2,1,0:T(8,128)(2,1)S(1)} %get-tuple-element.15), channel_id=1, source_target_pairs={{0,1},{1,0},{2,3},{3,2},{4,5},{5,4},{6,7},{7,6},{8,9},{9,8},{10,11... | collective-permute-start | bytes 1572872 | tf_op jit(solution)/shard_map/ppermute | solution.py:284
  57.7 2.0 %collective-permute-start.5 = (bf16[8,32,512]{2,1,0:T(8,128)(2,1)S(1)}, bf16[8,32,512]{2,1,0:T(8,128)(2,1)S(1)}, u32[]{:S(2)}, u32[]{:S(2)}) collective-permute-start(bf16[8,32,512]{2,1,0:T(8,128)(2,1)S(1)} %get-tuple-element.13), channel_id=1, source_target_pairs={{0,1},{1,0},{2,3},{3,2},{4,5},{5,4},{6,7},{7,6},{8,9},{9,8},{10,11... | collective-permute-start | bytes 786440 | tf_op jit(solution)/shard_map/ppermute | solution.py:285
  59.8 0.0 collective-permute-done.6.received
  59.8 0.1 shard_map.70
  59.9 3.4 %collective-permute-start.7 = (bf16[8,32,512]{2,1,0:T(8,128)(2,1)S(1)}, bf16[8,32,512]{2,1,0:T(8,128)(2,1)S(1)}, u32[]{:S(2)}, u32[]{:S(2)}) collective-permute-start(bf16[8,32,512]{2,1,0:T(8,128)(2,1)S(1)} %get-tuple-element.16), channel_id=1, source_target_pairs={{0,2},{2,0},{1,3},{3,1},{4,6},{6,4},{5,7},{7,5},{8,10},{10,8},{9,1... | collective-permute-start | bytes 786440 | tf_op jit(solution)/shard_map/ppermute | solution.py:291
  63.4 3.3 %collective-permute-start.8 = (bf16[4,32,512]{2,1,0:T(8,128)(2,1)S(1)}, bf16[4,32,512]{2,1,0:T(8,128)(2,1)S(1)}, u32[]{:S(2)}, u32[]{:S(2)}) collective-permute-start(bf16[4,32,512]{2,1,0:T(8,128)(2,1)S(1)} %get-tuple-element.17), channel_id=1, source_target_pairs={{32,0},{64,32},{96,64},{128,96},{160,128},{192,160},{224,192},{256... | collective-permute-start | bytes 393224 | tf_op jit(solution)/shard_map/ppermute | solution.py:292
  66.7 1.9 %collective-permute-start.9 = (bf16[4,32,512]{2,1,0:T(8,128)(2,1)S(1)}, bf16[4,32,512]{2,1,0:T(8,128)(2,1)S(1)}, u32[]{:S(2)}, u32[]{:S(2)}) collective-permute-start(bf16[4,32,512]{2,1,0:T(8,128)(2,1)S(1)} %get-tuple-element.18), channel_id=1, source_target_pairs={{32,2},{34,0},{64,34},{66,32},{96,66},{98,64},{128,98},{130,96},{1... | collective-permute-start | bytes 393224 | tf_op jit(solution)/shard_map/ppermute | solution.py:293
  68.6 0.0 collective-permute-done.5.partner
  68.6 3.5 %collective-permute-done.8.after = bf16[4,32,512]{2,1,0:T(8,128)(2,1)S(1)} collective-permute-done((bf16[4,32,512]{2,1,0:T(8,128)(2,1)S(1)}, bf16[4,32,512]{2,1,0:T(8,128)(2,1)S(1)}, u32[]{:S(2)}, u32[]{:S(2)}) %collective-permute-start.8) | collective-permute-done | bytes 131104 | tf_op jit(solution)/shard_map/ppermute | solution.py:292
  72.1 5.4 %collective-permute-done.9.after_across = bf16[4,32,512]{2,1,0:T(8,128)(2,1)S(1)} collective-permute-done((bf16[4,32,512]{2,1,0:T(8,128)(2,1)S(1)}, bf16[4,32,512]{2,1,0:T(8,128)(2,1)S(1)}, u32[]{:S(2)}, u32[]{:S(2)}) %collective-permute-start.9) | collective-permute-done | bytes 131104 | tf_op jit(solution)/shard_map/ppermute | solution.py:293
  77.5 0.0 collective-permute-done.7.across
  77.5 0.1 shard_map.71
  77.6 24.6 %all_to_all.15.pieces = bf16[8,32,1024]{2,1,0:T(8,128)(2,1)S(1)} all-to-all(bf16[8,32,1024]{2,1,0:T(8,128)(2,1)S(1)} %shard_map.71), channel_id=1, replica_groups=mesh['y'=8,'xlo'=2,'z'=8,'xhi'=2,'core'=2] {'z'}, dimensions={0} | all-to-all | bytes 1048576 | tf_op jit(solution)/shard_map/all_to_all | solution.py:240
  102.2 0.8 shard_map.72
  (1 shorter events, 0.0 us)
Async XLA Ops:
  2.4 10.5 %copy-start = (bf16[32,4096]{1,0:T(8,128)(2,1)S(1)}, bf16[32,4096]{1,0:T(8,128)(2,1)}, u32[]{:S(2)}) copy-start(bf16[32,4096]{1,0:T(8,128)(2,1)} %left.2) | copy-start | bytes 786436
  2.4 10.5 %copy-start.1 = (bf16[32,4096]{1,0:T(8,128)(2,1)S(1)}, bf16[32,4096]{1,0:T(8,128)(2,1)}, u32[]{:S(2)}) copy-start(bf16[32,4096]{1,0:T(8,128)(2,1)} %right.2) | copy-start | bytes 786436
  2.4 22.3 %all-to-all-start.1 = ((bf16[8,32,512]{2,1,0:T(8,128)(2,1)}), bf16[8,32,512]{2,1,0:T(8,128)(2,1)S(1)}, u32[]{:S(2)}, u32[]{:S(2)}) async-start(bf16[8,32,512]{2,1,0:T(8,128)(2,1)} %shard_map.68), calls=%async_computation.1 | async-start | bytes 524288 | tf_op jit(solution)/shard_map/all_to_all | solution.py:240
  24.7 26.0 %all-to-all-start = ((bf16[8,32,1024]{2,1,0:T(8,128)(2,1)}), bf16[8,32,1024]{2,1,0:T(8,128)(2,1)S(1)}, u32[]{:S(2)}, u32[]{:S(2)}) async-start(bf16[8,32,1024]{2,1,0:T(8,128)(2,1)} %shard_map.67), calls=%async_computation | async-start | bytes 1048576 | tf_op jit(solution)/shard_map/all_to_all | solution.py:240
  28.2 17.0 %collective-permute-start.1 = (bf16[8,32,512]{2,1,0:T(8,128)(2,1)S(1)}, bf16[8,32,512]{2,1,0:T(8,128)(2,1)S(1)}, u32[]{:S(2)}, u32[]{:S(2)}) collective-permute-start(bf16[8,32,512]{2,1,0:T(8,128)(2,1)S(1)} %all-to-all-done.1.own), channel_id=1, source_target_pairs={{0,2},{2,0},{1,3},{3,1},{4,6},{6,4},{5,7},{7,5},{8,10},{10,8},{9,1... | collective-permute-start | bytes 786440 | tf_op jit(solution)/shard_map/ppermute | solution.py:250
  33.2 10.4 %collective-permute-start.3 = (bf16[4,32,512]{2,1,0:T(8,128)(2,1)S(1)}, bf16[4,32,512]{2,1,0:T(8,128)(2,1)S(1)}, u32[]{:S(2)}, u32[]{:S(2)}) collective-permute-start(bf16[4,32,512]{2,1,0:T(8,128)(2,1)S(1)} %slice.5), channel_id=1, source_target_pairs={{0,34},{2,32},{32,66},{34,64},{64,98},{66,96},{96,130},{98,128},{1... | collective-permute-start | bytes 393224 | tf_op jit(solution)/shard_map/ppermute | solution.py:252
  36.3 9.0 %collective-permute-start.2 = (bf16[4,32,512]{2,1,0:T(8,128)(2,1)S(1)}, bf16[4,32,512]{2,1,0:T(8,128)(2,1)S(1)}, u32[]{:S(2)}, u32[]{:S(2)}) collective-permute-start(bf16[4,32,512]{2,1,0:T(8,128)(2,1)S(1)} %slice.5), channel_id=1, source_target_pairs={{0,32},{32,64},{64,96},{96,128},{128,160},{160,192},{192,224},{224... | collective-permute-start | bytes 393224 | tf_op jit(solution)/shard_map/ppermute | solution.py:251
  45.3 5.5 %collective-permute-start.4 = (bf16[16,32,512]{2,1,0:T(8,128)(2,1)S(1)}, bf16[16,32,512]{2,1,0:T(8,128)(2,1)S(1)}, u32[]{:S(2)}, u32[]{:S(2)}) collective-permute-start(bf16[16,32,512]{2,1,0:T(8,128)(2,1)S(1)} %pad_maximum_fusion), channel_id=1, source_target_pairs={{0,1},{1,0},{2,3},{3,2},{4,5},{5,4},{6,7},{7,6},{8,9},{9,8},{10,11... | collective-permute-start | bytes 1572872 | tf_op jit(solution)/shard_map/ppermute | solution.py:255
  47.2 3.6 %collective-permute-start = (bf16[8,32,512]{2,1,0:T(8,128)(2,1)S(1)}, bf16[8,32,512]{2,1,0:T(8,128)(2,1)S(1)}, u32[]{:S(2)}, u32[]{:S(2)}) collective-permute-start(bf16[8,32,512]{2,1,0:T(8,128)(2,1)S(1)} %all-to-all-done.1.own), channel_id=1, source_target_pairs={{0,1},{1,0},{2,3},{3,2},{4,5},{5,4},{6,7},{7,6},{8,9},{9,8},{10,11... | collective-permute-start | bytes 786440 | tf_op jit(solution)/shard_map/ppermute | solution.py:253
  55.4 4.3 %collective-permute-start.6 = (bf16[16,32,512]{2,1,0:T(8,128)(2,1)S(1)}, bf16[16,32,512]{2,1,0:T(8,128)(2,1)S(1)}, u32[]{:S(2)}, u32[]{:S(2)}) collective-permute-start(bf16[16,32,512]{2,1,0:T(8,128)(2,1)S(1)} %get-tuple-element.15), channel_id=1, source_target_pairs={{0,1},{1,0},{2,3},{3,2},{4,5},{5,4},{6,7},{7,6},{8,9},{9,8},{10,11... | collective-permute-start | bytes 1572872 | tf_op jit(solution)/shard_map/ppermute | solution.py:284
  57.7 10.9 %collective-permute-start.5 = (bf16[8,32,512]{2,1,0:T(8,128)(2,1)S(1)}, bf16[8,32,512]{2,1,0:T(8,128)(2,1)S(1)}, u32[]{:S(2)}, u32[]{:S(2)}) collective-permute-start(bf16[8,32,512]{2,1,0:T(8,128)(2,1)S(1)} %get-tuple-element.13), channel_id=1, source_target_pairs={{0,1},{1,0},{2,3},{3,2},{4,5},{5,4},{6,7},{7,6},{8,9},{9,8},{10,11... | collective-permute-start | bytes 786440 | tf_op jit(solution)/shard_map/ppermute | solution.py:285
  59.9 17.6 %collective-permute-start.7 = (bf16[8,32,512]{2,1,0:T(8,128)(2,1)S(1)}, bf16[8,32,512]{2,1,0:T(8,128)(2,1)S(1)}, u32[]{:S(2)}, u32[]{:S(2)}) collective-permute-start(bf16[8,32,512]{2,1,0:T(8,128)(2,1)S(1)} %get-tuple-element.16), channel_id=1, source_target_pairs={{0,2},{2,0},{1,3},{3,1},{4,6},{6,4},{5,7},{7,5},{8,10},{10,8},{9,1... | collective-permute-start | bytes 786440 | tf_op jit(solution)/shard_map/ppermute | solution.py:291
  63.4 8.8 %collective-permute-start.8 = (bf16[4,32,512]{2,1,0:T(8,128)(2,1)S(1)}, bf16[4,32,512]{2,1,0:T(8,128)(2,1)S(1)}, u32[]{:S(2)}, u32[]{:S(2)}) collective-permute-start(bf16[4,32,512]{2,1,0:T(8,128)(2,1)S(1)} %get-tuple-element.17), channel_id=1, source_target_pairs={{32,0},{64,32},{96,64},{128,96},{160,128},{192,160},{224,192},{256... | collective-permute-start | bytes 393224 | tf_op jit(solution)/shard_map/ppermute | solution.py:292
  66.7 10.8 %collective-permute-start.9 = (bf16[4,32,512]{2,1,0:T(8,128)(2,1)S(1)}, bf16[4,32,512]{2,1,0:T(8,128)(2,1)S(1)}, u32[]{:S(2)}, u32[]{:S(2)}) collective-permute-start(bf16[4,32,512]{2,1,0:T(8,128)(2,1)S(1)} %get-tuple-element.18), channel_id=1, source_target_pairs={{32,2},{34,0},{64,34},{66,32},{96,66},{98,64},{128,98},{130,96},{1... | collective-permute-start | bytes 393224 | tf_op jit(solution)/shard_map/ppermute | solution.py:293

commit v2 on v0

--- a/solution.py
+++ b/solution.py
@@ -17,6 +17,7 @@
 LINES = 16
 PIECE = 32
 PAIR = 672
+SHARED = PAIR - 256
 SPAN = 1536
 
 
@@ -127,8 +128,9 @@
             rows = slice(z * 64 + n * PIECE, z * 64 + n * PIECE + PIECE)
             qs[rows, :] = qg[z, :, n * 256 : n * 256 + 256]
             gs[rows, :] = qg[z, :, 512 + n * 256 : 768 + n * 256]
-    key_acc[...] = jnp.zeros_like(key_acc)
-    value_acc[...] = jnp.zeros_like(value_acc)
+    for acc in (key_acc, value_acc):
+        acc[0:96, :] = jnp.zeros((96, 256), jnp.float32)
+        acc[1440:SPAN, :] = jnp.zeros((96, 256), jnp.float32)
     offset = place[0] * 64 + place[1] * PIECE
     column = lax.broadcasted_iota(jnp.int32, (16, 128), 1)
     token = (column // 64) * 128 + (column & 31)
@@ -143,12 +145,11 @@
         dweights[...] = dot(values[window, :], grads, ((1,), (1,)))
         start = jnp.maximum(token + 1, jnp.where(place[2] == 0, 512 - low, 0))
 
-        def sums(step, carry):
+        def sums(allowed, step, carry):
             total, delta = carry
             rows = pl.ds(pl.multiple_of(step * 16, 16), 16)
             bent = jnp.tanh(scores[rows, :] * (SCALE / SOFTCAP))
-            row = key_row + step * 16
-            weight = jnp.where((row >= start) & (row <= stop), jnp.exp(SOFTCAP * bent), 0.0)
+            weight = jnp.where(allowed(key_row + step * 16), jnp.exp(SOFTCAP * bent), 0.0)
             scores[rows, :] = weight
             total = total + weight
             delta = delta + weight * dweights[rows, :]
@@ -156,7 +157,10 @@
             return total, delta
 
         zero = jnp.zeros((16, 128), jnp.float32)
-        total, delta = lax.fori_loop(0, PAIR // 16, sums, (zero, zero), unroll=21)
+        early = functools.partial(sums, lambda row: row >= start)
+        late = functools.partial(sums, lambda row: row <= stop)
+        total, delta = lax.fori_loop(0, 32, early, (zero, zero), unroll=16)
+        total, delta = lax.fori_loop(32, PAIR // 16, late, (total, delta), unroll=10)
         inverse = 1.0 / jnp.sum(total, axis=0, keepdims=True)
         delta = jnp.sum(delta, axis=0, keepdims=True) * inverse
         inverse = jnp.broadcast_to(inverse, (16, 128))
@@ -178,8 +182,15 @@
                 query_grad[pair * 2 + z, :, n * 256 : n * 256 + 256] = rows_grad[
                     first : first + PIECE, :
                 ]
-        key_acc[window, :] += dot(low_s[...], queries, ((1,), (0,)))
-        value_acc[window, :] += dot(low_w[...], grads, ((1,), (0,)))
+        for acc, terms in (
+            (key_acc, dot(low_s[...], queries, ((1,), (0,)))),
+            (value_acc, dot(low_w[...], grads, ((1,), (0,)))),
+        ):
+            if pair == 0:
+                acc[window, :] = terms
+            else:
+                acc[pl.ds(pl.multiple_of(low, PIECE), SHARED), :] += terms[0:SHARED, :]
+                acc[pl.ds(pl.multiple_of(low + SHARED, PIECE), 256), :] = terms[SHARED:PAIR, :]
 
     def take(target, idx, rows):
         target[idx, :, 0:256] = key_acc[rows, :].astype(target.dtype)

time: 110 us -> 109 us (level)
  no operation moved by 1% of the time
where the time goes in v2:
time: 109 us
  starting transfers between devices  55.5 us (51%)
  waiting for transfers between devices  39.2 us (36%)
  Pallas kernels  10.6 us (10%)
  local copies, waits for them, and re-layouts  2.37 us (2%)
    all_to_all x4, starting transfers between devices, exchange(): return lax.all_to_all(value, 'z', split_axis=0, concat_axis=0, tiled=True)  28.4 us
    all_to_all x4, waiting for transfers between devices, exchange(): return lax.all_to_all(value, 'z', split_axis=0, concat_axis=0, tiled=True)  22.1 us
    pallas_call x7, Pallas kernels, vmem_call(): pl.pallas_call(kernel, out_shape=out_shape, in_specs=[pl.BlockSpec(memory...  10.6 us
    ppermute x1, waiting for transfers between devices, shards(): before_across = lax.ppermute(own[4:8], CROSS, cross_perm(1))  5.45 us
    ppermute x1, waiting for transfers between devices, shards(): after_across = lax.ppermute(before_across, CROSS, cross_perm(-1))  5.38 us
    ppermute x1, starting transfers between devices, shards(): across = lax.ppermute(own, 'xhi', SWAP)  4.93 us
    ppermute x1, waiting for transfers between devices, shards(): after = lax.ppermute(before, LINE, line_perm(-1))  3.62 us
    ppermute x1, starting transfers between devices, shards(): across = lax.ppermute(across, 'xhi', SWAP)  3.45 us
  transfers between devices with their start and end apart: 14, of which 7 were waited for; matrix products, arithmetic and copies ran while one was open for 0% of the time, Pallas kernels for 3%

profile of v2, /device:TPU:32, one launch (start us, length us, event | category | flops | bytes accessed | tf_op | source)
XLA Modules:
  0.0 108.6 jit_solution(5046681498766187483)
XLA Ops:
  0.6 1.7 %shard_map.68 = bf16[8,32,512]{2,1,0:T(8,128)(2,1)} custom-call(bf16[32,2048]{1,0:T(8,128)(2,1)} %left.3, bf16[32,2048]{1,0:T(8,128)(2,1)} %right.3), custom_call_target="tpu_custom_call" | custom-call | bytes 524288 | tf_op jit(solution)/shard_map/pallas_call | solution.py:45
  2.4 0.0 copy-start
  2.4 0.0 copy-start.1
  2.4 10.5 %all-to-all-start.1 = ((bf16[8,32,512]{2,1,0:T(8,128)(2,1)}), bf16[8,32,512]{2,1,0:T(8,128)(2,1)S(1)}, u32[]{:S(2)}, u32[]{:S(2)}) async-start(bf16[8,32,512]{2,1,0:T(8,128)(2,1)} %shard_map.68), calls=%async_computation.1 | async-start | bytes 524288 | tf_op jit(solution)/shard_map/all_to_all | solution.py:243
  12.9 0.0 copy-done
  12.9 0.0 copy-done.1
  12.9 1.1 %shard_map.67 = bf16[8,32,1024]{2,1,0:T(8,128)(2,1)} custom-call(bf16[32,4096]{1,0:T(8,128)(2,1)S(1)} %copy-done, bf16[32,4096]{1,0:T(8,128)(2,1)S(1)} %copy-done.1), custom_call_target="tpu_custom_call" | custom-call | bytes 1048576 | tf_op jit(solution)/shard_map/pallas_call | solution.py:45
  14.0 10.7 %all-to-all-done.1.own = bf16[8,32,512]{2,1,0:T(8,128)(2,1)S(1)} async-done(((bf16[8,32,512]{2,1,0:T(8,128)(2,1)}), bf16[8,32,512]{2,1,0:T(8,128)(2,1)S(1)}, u32[]{:S(2)}, u32[]{:S(2)}) %all-to-all-start.1) | async-done | bytes 262176 | tf_op jit(solution)/shard_map/all_to_all | solution.py:243
  24.7 3.5 %all-to-all-start = ((bf16[8,32,1024]{2,1,0:T(8,128)(2,1)}), bf16[8,32,1024]{2,1,0:T(8,128)(2,1)S(1)}, u32[]{:S(2)}, u32[]{:S(2)}) async-start(bf16[8,32,1024]{2,1,0:T(8,128)(2,1)} %shard_map.67), calls=%async_computation | async-start | bytes 1048576 | tf_op jit(solution)/shard_map/all_to_all | solution.py:243
  28.2 4.9 %collective-permute-start.1 = (bf16[8,32,512]{2,1,0:T(8,128)(2,1)S(1)}, bf16[8,32,512]{2,1,0:T(8,128)(2,1)S(1)}, u32[]{:S(2)}, u32[]{:S(2)}) collective-permute-start(bf16[8,32,512]{2,1,0:T(8,128)(2,1)S(1)} %all-to-all-done.1.own), channel_id=1, source_target_pairs={{0,2},{2,0},{1,3},{3,1},{4,6},{6,4},{5,7},{7,5},{8,10},{10,8},{9,1... | collective-permute-start | bytes 786440 | tf_op jit(solution)/shard_map/ppermute | solution.py:253
  33.2 3.0 %collective-permute-start.3 = (bf16[4,32,512]{2,1,0:T(8,128)(2,1)S(1)}, bf16[4,32,512]{2,1,0:T(8,128)(2,1)S(1)}, u32[]{:S(2)}, u32[]{:S(2)}) collective-permute-start(bf16[4,32,512]{2,1,0:T(8,128)(2,1)S(1)} %slice.5), channel_id=1, source_target_pairs={{0,34},{2,32},{32,66},{34,64},{64,98},{66,96},{96,130},{98,128},{1... | collective-permute-start | bytes 393224 | tf_op jit(solution)/shard_map/ppermute | solution.py:255
  36.3 1.9 %collective-permute-start.2 = (bf16[4,32,512]{2,1,0:T(8,128)(2,1)S(1)}, bf16[4,32,512]{2,1,0:T(8,128)(2,1)S(1)}, u32[]{:S(2)}, u32[]{:S(2)}) collective-permute-start(bf16[4,32,512]{2,1,0:T(8,128)(2,1)S(1)} %slice.5), channel_id=1, source_target_pairs={{0,32},{32,64},{64,96},{96,128},{128,160},{160,192},{192,224},{224... | collective-permute-start | bytes 393224 | tf_op jit(solution)/shard_map/ppermute | solution.py:254
  38.2 5.5 %collective-permute-done.3.before_across = bf16[4,32,512]{2,1,0:T(8,128)(2,1)S(1)} collective-permute-done((bf16[4,32,512]{2,1,0:T(8,128)(2,1)S(1)}, bf16[4,32,512]{2,1,0:T(8,128)(2,1)S(1)}, u32[]{:S(2)}, u32[]{:S(2)}) %collective-permute-start.3) | collective-permute-done | bytes 131104 | tf_op jit(solution)/shard_map/ppermute | solution.py:255
  43.6 1.6 %collective-permute-done.2.before = bf16[4,32,512]{2,1,0:T(8,128)(2,1)S(1)} collective-permute-done((bf16[4,32,512]{2,1,0:T(8,128)(2,1)S(1)}, bf16[4,32,512]{2,1,0:T(8,128)(2,1)S(1)}, u32[]{:S(2)}, u32[]{:S(2)}) %collective-permute-start.2) | collective-permute-done | bytes 131104 | tf_op jit(solution)/shard_map/ppermute | solution.py:254
  45.2 0.0 collective-permute-done.1.across
  45.2 0.1 pad_maximum_fusion
  45.3 1.9 %collective-permute-start.4 = (bf16[16,32,512]{2,1,0:T(8,128)(2,1)S(1)}, bf16[16,32,512]{2,1,0:T(8,128)(2,1)S(1)}, u32[]{:S(2)}, u32[]{:S(2)}) collective-permute-start(bf16[16,32,512]{2,1,0:T(8,128)(2,1)S(1)} %pad_maximum_fusion), channel_id=1, source_target_pairs={{0,1},{1,0},{2,3},{3,2},{4,5},{5,4},{6,7},{7,6},{8,9},{9,8},{10,11... | collective-permute-start | bytes 1572872 | tf_op jit(solution)/shard_map/ppermute | solution.py:258
  47.2 2.4 %collective-permute-start = (bf16[8,32,512]{2,1,0:T(8,128)(2,1)S(1)}, bf16[8,32,512]{2,1,0:T(8,128)(2,1)S(1)}, u32[]{:S(2)}, u32[]{:S(2)}) collective-permute-start(bf16[8,32,512]{2,1,0:T(8,128)(2,1)S(1)} %all-to-all-done.1.own), channel_id=1, source_target_pairs={{0,1},{1,0},{2,3},{3,2},{4,5},{5,4},{6,7},{7,6},{8,9},{9,8},{10,11... | collective-permute-start | bytes 786440 | tf_op jit(solution)/shard_map/ppermute | solution.py:256
  49.6 0.1 pad_add_fusion.place
  49.7 1.1 collective-permute-done.partner
  50.8 0.0 copy-start.2
  50.8 0.7 copy-done.2
  51.5 0.0 all-to-all-done.qg
  51.5 0.0 collective-permute-done.4.reach
  51.5 0.0 copy-start.3
  51.5 0.9 copy-done.3
  52.4 5.4 %shard_map.69 = (bf16[8,32,512]{2,1,0:T(8,128)(2,1)}, f32[8,32,512]{2,1,0:T(8,128)S(1)}, f32[16,32,512]{2,1,0:T(8,128)S(1)}, bf16[8,32,512]{2,1,0:T(8,128)(2,1)S(1)}, bf16[16,32,512]{2,1,0:T(8,128)(2,1)}) custom-call(s32[3]{0:T(128)S(1)} %pad_add_fusion.place, bf16[8,32,1024]{2,1,0:T(8,128)(2,1)S(1)} %all-to-all-done.qg, ...), custom_call_target="tpu_custom_call" | custom-call | flops 880803840 | bytes 4718604 | tf_op jit(solution)/shard_map/pallas_call | solution.py:45
  57.8 0.7 copy-done.4
  58.5 2.3 %collective-permute-start.6 = (bf16[16,32,512]{2,1,0:T(8,128)(2,1)}, bf16[16,32,512]{2,1,0:T(8,128)(2,1)S(1)}, u32[]{:S(2)}, u32[]{:S(2)}) collective-permute-start(bf16[16,32,512]{2,1,0:T(8,128)(2,1)} %get-tuple-element.17), channel_id=1, source_target_pairs={{0,1},{1,0},{2,3},{3,2},{4,5},{5,4},{6,7},{7,6},{8,9},{9,8},{10,11... | collective-permute-start | bytes 1572872 | tf_op jit(solution)/shard_map/ppermute | solution.py:287
  60.8 0.0 copy-start.5
  60.8 7.3 %all-to-all-start.2 = ((bf16[8,32,512]{2,1,0:T(8,128)(2,1)}), bf16[8,32,512]{2,1,0:T(8,128)(2,1)S(1)}, u32[]{:S(2)}, u32[]{:S(2)}) async-start(bf16[8,32,512]{2,1,0:T(8,128)(2,1)} %get-tuple-element.13), calls=%async_computation.2 | async-start | bytes 524288 | tf_op jit(solution)/shard_map/all_to_all | solution.py:243
  68.1 0.0 copy-done.5
  68.1 1.9 %collective-permute-start.5 = (bf16[8,32,512]{2,1,0:T(8,128)(2,1)S(1)}, bf16[8,32,512]{2,1,0:T(8,128)(2,1)S(1)}, u32[]{:S(2)}, u32[]{:S(2)}) collective-permute-start(bf16[8,32,512]{2,1,0:T(8,128)(2,1)S(1)} %copy-done.5), channel_id=1, source_target_pairs={{0,1},{1,0},{2,3},{3,2},{4,5},{5,4},{6,7},{7,6},{8,9},{9,8},{10,11... | collective-permute-start | bytes 786440 | tf_op jit(solution)/shard_map/ppermute | solution.py:288
  70.0 0.0 collective-permute-done.6.received
  70.0 0.1 shard_map.71
  70.1 3.5 %collective-permute-start.7 = (bf16[8,32,512]{2,1,0:T(8,128)(2,1)S(1)}, bf16[8,32,512]{2,1,0:T(8,128)(2,1)S(1)}, u32[]{:S(2)}, u32[]{:S(2)}) collective-permute-start(bf16[8,32,512]{2,1,0:T(8,128)(2,1)S(1)} %get-tuple-element.18), channel_id=1, source_target_pairs={{0,2},{2,0},{1,3},{3,1},{4,6},{6,4},{5,7},{7,5},{8,10},{10,8},{9,1... | collective-permute-start | bytes 786440 | tf_op jit(solution)/shard_map/ppermute | solution.py:294
  73.6 3.3 %collective-permute-start.8 = (bf16[4,32,512]{2,1,0:T(8,128)(2,1)S(1)}, bf16[4,32,512]{2,1,0:T(8,128)(2,1)S(1)}, u32[]{:S(2)}, u32[]{:S(2)}) collective-permute-start(bf16[4,32,512]{2,1,0:T(8,128)(2,1)S(1)} %get-tuple-element.19), channel_id=1, source_target_pairs={{32,0},{64,32},{96,64},{128,96},{160,128},{192,160},{224,192},{256... | collective-permute-start | bytes 393224 | tf_op jit(solution)/shard_map/ppermute | solution.py:295
  76.9 1.9 %collective-permute-start.9 = (bf16[4,32,512]{2,1,0:T(8,128)(2,1)S(1)}, bf16[4,32,512]{2,1,0:T(8,128)(2,1)S(1)}, u32[]{:S(2)}, u32[]{:S(2)}) collective-permute-start(bf16[4,32,512]{2,1,0:T(8,128)(2,1)S(1)} %get-tuple-element.20), channel_id=1, source_target_pairs={{32,2},{34,0},{64,34},{66,32},{96,66},{98,64},{128,98},{130,96},{1... | collective-permute-start | bytes 393224 | tf_op jit(solution)/shard_map/ppermute | solution.py:296
  78.8 0.0 collective-permute-done.5.partner
  78.8 3.6 %collective-permute-done.8.after = bf16[4,32,512]{2,1,0:T(8,128)(2,1)S(1)} collective-permute-done((bf16[4,32,512]{2,1,0:T(8,128)(2,1)S(1)}, bf16[4,32,512]{2,1,0:T(8,128)(2,1)S(1)}, u32[]{:S(2)}, u32[]{:S(2)}) %collective-permute-start.8) | collective-permute-done | bytes 131104 | tf_op jit(solution)/shard_map/ppermute | solution.py:295
  82.4 5.4 %collective-permute-done.9.after_across = bf16[4,32,512]{2,1,0:T(8,128)(2,1)S(1)} collective-permute-done((bf16[4,32,512]{2,1,0:T(8,128)(2,1)S(1)}, bf16[4,32,512]{2,1,0:T(8,128)(2,1)S(1)}, u32[]{:S(2)}, u32[]{:S(2)}) %collective-permute-start.9) | collective-permute-done | bytes 131104 | tf_op jit(solution)/shard_map/ppermute | solution.py:296
  87.8 0.0 collective-permute-done.7.across
  87.8 0.8 shard_map.72
  88.6 0.0 all-to-all-done.2.pieces
  88.6 7.2 %all-to-all-start.3 = ((bf16[8,32,512]{2,1,0:T(8,128)(2,1)}), bf16[8,32,512]{2,1,0:T(8,128)(2,1)S(1)}, u32[]{:S(2)}, u32[]{:S(2)}) async-start(bf16[8,32,512]{2,1,0:T(8,128)(2,1)} %shard_map.72), calls=%async_computation.3 | async-start | bytes 524288 | tf_op jit(solution)/shard_map/all_to_all | solution.py:243
  95.8 0.7 shard_map.70
  96.6 11.3 %all-to-all-done.3.pieces = bf16[8,32,512]{2,1,0:T(8,128)(2,1)S(1)} async-done(((bf16[8,32,512]{2,1,0:T(8,128)(2,1)}), bf16[8,32,512]{2,1,0:T(8,128)(2,1)S(1)}, u32[]{:S(2)}, u32[]{:S(2)}) %all-to-all-start.3) | async-done | bytes 262176 | tf_op jit(solution)/shard_map/all_to_all | solution.py:243
  107.9 0.7 shard_map.73
  (2 shorter events, 0.0 us)
Async XLA Ops:
  2.4 10.5 %copy-start = (bf16[32,4096]{1,0:T(8,128)(2,1)S(1)}, bf16[32,4096]{1,0:T(8,128)(2,1)}, u32[]{:S(2)}) copy-start(bf16[32,4096]{1,0:T(8,128)(2,1)} %left.2) | copy-start | bytes 786436
  2.4 10.5 %copy-start.1 = (bf16[32,4096]{1,0:T(8,128)(2,1)S(1)}, bf16[32,4096]{1,0:T(8,128)(2,1)}, u32[]{:S(2)}) copy-start(bf16[32,4096]{1,0:T(8,128)(2,1)} %right.2) | copy-start | bytes 786436
  2.4 22.3 %all-to-all-start.1 = ((bf16[8,32,512]{2,1,0:T(8,128)(2,1)}), bf16[8,32,512]{2,1,0:T(8,128)(2,1)S(1)}, u32[]{:S(2)}, u32[]{:S(2)}) async-start(bf16[8,32,512]{2,1,0:T(8,128)(2,1)} %shard_map.68), calls=%async_computation.1 | async-start | bytes 524288 | tf_op jit(solution)/shard_map/all_to_all | solution.py:243
  24.7 26.7 %all-to-all-start = ((bf16[8,32,1024]{2,1,0:T(8,128)(2,1)}), bf16[8,32,1024]{2,1,0:T(8,128)(2,1)S(1)}, u32[]{:S(2)}, u32[]{:S(2)}) async-start(bf16[8,32,1024]{2,1,0:T(8,128)(2,1)} %shard_map.67), calls=%async_computation | async-start | bytes 1048576 | tf_op jit(solution)/shard_map/all_to_all | solution.py:243
  28.2 17.0 %collective-permute-start.1 = (bf16[8,32,512]{2,1,0:T(8,128)(2,1)S(1)}, bf16[8,32,512]{2,1,0:T(8,128)(2,1)S(1)}, u32[]{:S(2)}, u32[]{:S(2)}) collective-permute-start(bf16[8,32,512]{2,1,0:T(8,128)(2,1)S(1)} %all-to-all-done.1.own), channel_id=1, source_target_pairs={{0,2},{2,0},{1,3},{3,1},{4,6},{6,4},{5,7},{7,5},{8,10},{10,8},{9,1... | collective-permute-start | bytes 786440 | tf_op jit(solution)/shard_map/ppermute | solution.py:253
  33.2 10.4 %collective-permute-start.3 = (bf16[4,32,512]{2,1,0:T(8,128)(2,1)S(1)}, bf16[4,32,512]{2,1,0:T(8,128)(2,1)S(1)}, u32[]{:S(2)}, u32[]{:S(2)}) collective-permute-start(bf16[4,32,512]{2,1,0:T(8,128)(2,1)S(1)} %slice.5), channel_id=1, source_target_pairs={{0,34},{2,32},{32,66},{34,64},{64,98},{66,96},{96,130},{98,128},{1... | collective-permute-start | bytes 393224 | tf_op jit(solution)/shard_map/ppermute | solution.py:255
  36.3 9.0 %collective-permute-start.2 = (bf16[4,32,512]{2,1,0:T(8,128)(2,1)S(1)}, bf16[4,32,512]{2,1,0:T(8,128)(2,1)S(1)}, u32[]{:S(2)}, u32[]{:S(2)}) collective-permute-start(bf16[4,32,512]{2,1,0:T(8,128)(2,1)S(1)} %slice.5), channel_id=1, source_target_pairs={{0,32},{32,64},{64,96},{96,128},{128,160},{160,192},{192,224},{224... | collective-permute-start | bytes 393224 | tf_op jit(solution)/shard_map/ppermute | solution.py:254
  45.3 6.2 %collective-permute-start.4 = (bf16[16,32,512]{2,1,0:T(8,128)(2,1)S(1)}, bf16[16,32,512]{2,1,0:T(8,128)(2,1)S(1)}, u32[]{:S(2)}, u32[]{:S(2)}) collective-permute-start(bf16[16,32,512]{2,1,0:T(8,128)(2,1)S(1)} %pad_maximum_fusion), channel_id=1, source_target_pairs={{0,1},{1,0},{2,3},{3,2},{4,5},{5,4},{6,7},{7,6},{8,9},{9,8},{10,11... | collective-permute-start | bytes 1572872 | tf_op jit(solution)/shard_map/ppermute | solution.py:258
  47.2 3.6 %collective-permute-start = (bf16[8,32,512]{2,1,0:T(8,128)(2,1)S(1)}, bf16[8,32,512]{2,1,0:T(8,128)(2,1)S(1)}, u32[]{:S(2)}, u32[]{:S(2)}) collective-permute-start(bf16[8,32,512]{2,1,0:T(8,128)(2,1)S(1)} %all-to-all-done.1.own), channel_id=1, source_target_pairs={{0,1},{1,0},{2,3},{3,2},{4,5},{5,4},{6,7},{7,6},{8,9},{9,8},{10,11... | collective-permute-start | bytes 786440 | tf_op jit(solution)/shard_map/ppermute | solution.py:256
  50.8 0.7 copy-start.2
  51.5 1.0 copy-start.3
  57.8 0.7 copy-start.4
  58.5 11.5 %collective-permute-start.6 = (bf16[16,32,512]{2,1,0:T(8,128)(2,1)}, bf16[16,32,512]{2,1,0:T(8,128)(2,1)S(1)}, u32[]{:S(2)}, u32[]{:S(2)}) collective-permute-start(bf16[16,32,512]{2,1,0:T(8,128)(2,1)} %get-tuple-element.17), channel_id=1, source_target_pairs={{0,1},{1,0},{2,3},{3,2},{4,5},{5,4},{6,7},{7,6},{8,9},{9,8},{10,11... | collective-permute-start | bytes 1572872 | tf_op jit(solution)/shard_map/ppermute | solution.py:287
  60.8 7.3 %copy-start.5 = (bf16[8,32,512]{2,1,0:T(8,128)(2,1)S(1)}, bf16[8,32,512]{2,1,0:T(8,128)(2,1)}, u32[]{:S(2)}) copy-start(bf16[8,32,512]{2,1,0:T(8,128)(2,1)} %copy-done.4) | copy-start | bytes 786436
  60.8 27.9 %all-to-all-start.2 = ((bf16[8,32,512]{2,1,0:T(8,128)(2,1)}), bf16[8,32,512]{2,1,0:T(8,128)(2,1)S(1)}, u32[]{:S(2)}, u32[]{:S(2)}) async-start(bf16[8,32,512]{2,1,0:T(8,128)(2,1)} %get-tuple-element.13), calls=%async_computation.2 | async-start | bytes 524288 | tf_op jit(solution)/shard_map/all_to_all | solution.py:243
  68.1 10.8 %collective-permute-start.5 = (bf16[8,32,512]{2,1,0:T(8,128)(2,1)S(1)}, bf16[8,32,512]{2,1,0:T(8,128)(2,1)S(1)}, u32[]{:S(2)}, u32[]{:S(2)}) collective-permute-start(bf16[8,32,512]{2,1,0:T(8,128)(2,1)S(1)} %copy-done.5), channel_id=1, source_target_pairs={{0,1},{1,0},{2,3},{3,2},{4,5},{5,4},{6,7},{7,6},{8,9},{9,8},{10,11... | collective-permute-start | bytes 786440 | tf_op jit(solution)/shard_map/ppermute | solution.py:288
  70.1 17.7 %collective-permute-start.7 = (bf16[8,32,512]{2,1,0:T(8,128)(2,1)S(1)}, bf16[8,32,512]{2,1,0:T(8,128)(2,1)S(1)}, u32[]{:S(2)}, u32[]{:S(2)}) collective-permute-start(bf16[8,32,512]{2,1,0:T(8,128)(2,1)S(1)} %get-tuple-element.18), channel_id=1, source_target_pairs={{0,2},{2,0},{1,3},{3,1},{4,6},{6,4},{5,7},{7,5},{8,10},{10,8},{9,1... | collective-permute-start | bytes 786440 | tf_op jit(solution)/shard_map/ppermute | solution.py:294
  73.6 8.9 %collective-permute-start.8 = (bf16[4,32,512]{2,1,0:T(8,128)(2,1)S(1)}, bf16[4,32,512]{2,1,0:T(8,128)(2,1)S(1)}, u32[]{:S(2)}, u32[]{:S(2)}) collective-permute-start(bf16[4,32,512]{2,1,0:T(8,128)(2,1)S(1)} %get-tuple-element.19), channel_id=1, source_target_pairs={{32,0},{64,32},{96,64},{128,96},{160,128},{192,160},{224,192},{256... | collective-permute-start | bytes 393224 | tf_op jit(solution)/shard_map/ppermute | solution.py:295
  76.9 10.9 %collective-permute-start.9 = (bf16[4,32,512]{2,1,0:T(8,128)(2,1)S(1)}, bf16[4,32,512]{2,1,0:T(8,128)(2,1)S(1)}, u32[]{:S(2)}, u32[]{:S(2)}) collective-permute-start(bf16[4,32,512]{2,1,0:T(8,128)(2,1)S(1)} %get-tuple-element.20), channel_id=1, source_target_pairs={{32,2},{34,0},{64,34},{66,32},{96,66},{98,64},{128,98},{130,96},{1... | collective-permute-start | bytes 393224 | tf_op jit(solution)/shard_map/ppermute | solution.py:296
  88.6 19.3 %all-to-all-start.3 = ((bf16[8,32,512]{2,1,0:T(8,128)(2,1)}), bf16[8,32,512]{2,1,0:T(8,128)(2,1)S(1)}, u32[]{:S(2)}, u32[]{:S(2)}) async-start(bf16[8,32,512]{2,1,0:T(8,128)(2,1)} %shard_map.72), calls=%async_computation.3 | async-start | bytes 524288 | tf_op jit(solution)/shard_map/all_to_all | solution.py:243
